TPU v7x, 32 devices: a whole 2x2x4 slice. The times are simulated.
32 devices in a mesh: tower: 2 (over x), dp: 16 (over z, y, core).
Axes of the slice: x: 2, y: 2, z: 4, core: 2. Of those that a mesh axis runs over, the one named last changes fastest.
Arguments:
- images: bfloat16 [288, 50, 768], P('dp'), may hold values from -6 to 6
- captions: bfloat16 [864, 16, 768], P('dp'), may hold values from -6 to 6
- token_ids: int32 [864, 16], P('dp'), may hold values from 0 to 31999, as said below
- counts: int32 [288], P('dp'), may hold values from 1 to 5, as said below
- matches: int32 [864], P('dp'), may hold values from 0 to 287, as said below
- image_weights: bfloat16 [9216, 768], P('dp')
- image_norms: float32 [4, 768], replicated, may hold values from -1.2 to 1.2, as said below
- weights: float32 [9216, 768], P(('tower', 'dp'))
- norm_params: float32 [4, 768], replicated, may hold values from -1.2 to 1.2, as said below
- momentum: float32 [9216, 768], P(('tower', 'dp'))
- norm_momentum: float32 [4, 768], replicated
- averages: float32 [9216, 768], P(('tower', 'dp'))
- norm_averages: float32 [4, 768], replicated, may hold values from -1.2 to 1.2
Outputs:
- grads: float32 [9216, 768], P(('tower', 'dp'))
- norm_grads: float32 [4, 768], replicated
- input_grad: float32 [864, 16, 768], P('dp', None, 'tower')
- new_weights: float32 [9216, 768], P(('tower', 'dp'))
- new_momentum: float32 [9216, 768], P(('tower', 'dp'))
- new_averages: float32 [9216, 768], P(('tower', 'dp'))
- new_norm_params: float32 [4, 768], replicated
- new_norm_momentum: float32 [4, 768], replicated
- new_norm_averages: float32 [4, 768], replicated
- grad_norm: float32 [], replicated
Inputs may be any that keep to these rules, and one draw needn't show every extreme that they name: `token_ids`: in each caption the ids are nonzero on a leading run of 4 to 16 positions and 0 after it. counts[i] is the number of captions c with matches[c] = i; the counts sum to 864. `matches`: image i is named by exactly counts[i] captions. `norm_params`: rows 0 and 2 are gains, rows 1 and 3 biases. `image_norms`: rows 0 and 2 are gains, rows 1 and 3 biases.
All inputs are finite; a program needn't handle non-finite values.
Results may differ from a plain program's by a relative error of at most 0.014.
The roundings to bfloat16 on the way count: a program that leaves them out, or rounds other values in their place, can miss the bound.
Values may be sent and summed in bfloat16 or wider, within the bound.
No kernel may reach another device: no remote copies, remote signals or barrier semaphores. Data moves between devices by JAX's collectives and lax.ppermute only.
A program may use at most 320 MiB of HBM per device.

v0:
```python
from functools import partial
import math
import jax
import jax.numpy as jnp
from jax import lax
from jax.sharding import PartitionSpec as P

HEADS = 12
EPSILON = 1e-06
LOGIT_SCALE = 50.0
CLIP_NORM = 1.0
MOMENTUM_RATE = 0.9
DECAY_RATE = 0.0001
AVERAGE_RATE = 0.7


def passed_along(block, axis, distance):
    devices = range(lax.axis_size(axis))
    route = [(i - distance, i) for i in devices if i - distance in devices]
    return lax.ppermute(block, axis, route)


def layer_norm(rows_in, scaling, offset):
    middle = jnp.mean(rows_in, axis=-1, keepdims=True)
    centred = rows_in - middle
    spread = jnp.mean(centred * centred, axis=-1, keepdims=True)
    return centred * lax.rsqrt(spread + EPSILON) * scaling + offset


def split_packed(packed):
    features = packed.shape[1]
    hidden_units = (packed.shape[0] - 4 * features) // 2
    return (
        packed[: 3 * features],
        packed[3 * features : 4 * features],
        packed[4 * features : 4 * features + hidden_units],
        packed[4 * features + hidden_units :],
    )


def masked_scores(queries, key_rows, causal):
    scores = jnp.einsum(
        "nqhd,nkhd->nhqk", queries, key_rows, preferred_element_type=jnp.float32
    ) * queries.shape[-1] ** (-0.5)
    if causal:
        seq_length = queries.shape[1]
        causal_mask = lax.broadcasted_iota(
            jnp.int32, (seq_length, seq_length), 0
        ) >= lax.broadcasted_iota(jnp.int32, (seq_length, seq_length), 1)
        scores = jnp.where(causal_mask, scores, -1e30)
    return scores


def block_forward(rows_in, packed, norms, causal):
    qkv_matrix, out_matrix, up_matrix, down_matrix = split_packed(packed)
    seq_count, seq_length, features = rows_in.shape
    normed = layer_norm(rows_in, norms[0], norms[1]).astype(jnp.bfloat16)
    joined = jnp.einsum(
        "nld,ed->nle", normed, qkv_matrix, preferred_element_type=jnp.float32
    ).astype(jnp.bfloat16)
    joined = joined.reshape(seq_count, seq_length, 3, HEADS, features // HEADS)
    scores = masked_scores(joined[:, :, 0], joined[:, :, 1], causal)
    highest = jnp.max(scores, axis=-1, keepdims=True)
    exponent = jnp.exp(scores - highest)
    totals = jnp.sum(exponent, axis=-1, keepdims=True)
    attn_probs = (exponent / totals).astype(jnp.bfloat16)
    log_total = highest + jnp.log(totals)
    attended = jnp.einsum(
        "nhqk,nkhd->nqhd", attn_probs, joined[:, :, 2], preferred_element_type=jnp.float32
    )
    attended = attended.astype(jnp.bfloat16).reshape(seq_count, seq_length, features)
    hidden = rows_in + jnp.einsum(
        "nld,ed->nle", attended, out_matrix, preferred_element_type=jnp.float32
    )
    normed_mid = layer_norm(hidden, norms[2], norms[3]).astype(jnp.bfloat16)
    pre_act = jnp.einsum("nld,fd->nlf", normed_mid, up_matrix, preferred_element_type=jnp.float32)
    activated = jax.nn.gelu(pre_act, approximate=True).astype(jnp.bfloat16)
    block_out = hidden + jnp.einsum(
        "nlf,fd->nld", activated, down_matrix, preferred_element_type=jnp.float32
    )
    return (
        (normed, joined, log_total, attended, hidden, normed_mid, pre_act, activated),
        block_out,
    )


def block_backward(grad_rows, rows_in, packed, norms, kept):
    normed, joined, log_total, attended, hidden, normed_mid, pre_act, activated = kept
    qkv_matrix, out_matrix, up_matrix, down_matrix = split_packed(packed)
    seq_count, seq_length, features = rows_in.shape
    queries, key_rows, values = (joined[:, :, 0], joined[:, :, 1], joined[:, :, 2])
    grad_branch = grad_rows.astype(jnp.bfloat16)
    grad_down_matrix = jnp.einsum(
        "nlf,nld->fd", activated, grad_branch, preferred_element_type=jnp.float32
    )
    grad_act = jnp.einsum(
        "nld,fd->nlf", grad_branch, down_matrix, preferred_element_type=jnp.float32
    ).astype(jnp.bfloat16)
    gelu_pull = jax.vjp(partial(jax.nn.gelu, approximate=True), pre_act)[1]
    grad_pre = gelu_pull(grad_act.astype(jnp.float32))[0].astype(jnp.bfloat16)
    grad_up_matrix = jnp.einsum(
        "nlf,nld->fd", grad_pre, normed_mid, preferred_element_type=jnp.float32
    )
    grad_normed_mid = jnp.einsum(
        "nlf,fd->nld", grad_pre, up_matrix, preferred_element_type=jnp.float32
    )
    mid_pull = jax.vjp(layer_norm, hidden, norms[2], norms[3])[1]
    grad_mid_part, grad_gain_mid, grad_shift_mid = mid_pull(grad_normed_mid)
    grad_hidden = grad_rows + grad_mid_part
    grad_mixed = grad_hidden.astype(jnp.bfloat16)
    grad_out_matrix = jnp.einsum(
        "nle,nld->ed", grad_mixed, attended, preferred_element_type=jnp.float32
    )
    grad_att = jnp.einsum(
        "nle,ed->nld", grad_mixed, out_matrix, preferred_element_type=jnp.float32
    ).astype(jnp.bfloat16)
    grad_att = grad_att.reshape(seq_count, seq_length, HEADS, features // HEADS)
    attn_probs = jnp.exp(masked_scores(queries, key_rows, True) - log_total)
    grad_probs = jnp.einsum("nqhd,nkhd->nhqk", grad_att, values, preferred_element_type=jnp.float32)
    grad_values = jnp.einsum(
        "nhqk,nqhd->nkhd",
        attn_probs.astype(jnp.bfloat16),
        grad_att,
        preferred_element_type=jnp.float32,
    )
    grad_scores = attn_probs * (
        grad_probs - jnp.sum(attn_probs * grad_probs, axis=-1, keepdims=True)
    )
    grad_raw = (grad_scores * queries.shape[-1] ** (-0.5)).astype(jnp.bfloat16)
    grad_queries = jnp.einsum(
        "nhqk,nkhd->nqhd", grad_raw, key_rows, preferred_element_type=jnp.float32
    )
    grad_keys = jnp.einsum("nhqk,nqhd->nkhd", grad_raw, queries, preferred_element_type=jnp.float32)
    grad_joined = jnp.stack([grad_queries, grad_keys, grad_values], axis=2).astype(jnp.bfloat16)
    grad_joined = grad_joined.reshape(seq_count, seq_length, 3 * features)
    grad_qkv_matrix = jnp.einsum(
        "nle,nld->ed", grad_joined, normed, preferred_element_type=jnp.float32
    )
    grad_normed = jnp.einsum(
        "nle,ed->nld", grad_joined, qkv_matrix, preferred_element_type=jnp.float32
    )
    first_pull = jax.vjp(layer_norm, rows_in, norms[0], norms[1])[1]
    grad_first, grad_gain_first, grad_shift_first = first_pull(grad_normed)
    matrix_grads = jnp.concatenate(
        [grad_qkv_matrix, grad_out_matrix, grad_up_matrix, grad_down_matrix], axis=0
    )
    small_grads = jnp.stack([grad_gain_first, grad_shift_first, grad_gain_mid, grad_shift_mid])
    return (matrix_grads, small_grads, grad_hidden + grad_first)


def text_blank(seq_count, seq_length, features, hidden_units):
    return (
        jnp.zeros((seq_count, seq_length, features), jnp.bfloat16),
        jnp.zeros((seq_count, seq_length, 3, HEADS, features // HEADS), jnp.bfloat16),
        jnp.zeros((seq_count, HEADS, seq_length, 1), jnp.float32),
        jnp.zeros((seq_count, seq_length, features), jnp.bfloat16),
        jnp.zeros((seq_count, seq_length, features), jnp.float32),
        jnp.zeros((seq_count, seq_length, features), jnp.bfloat16),
        jnp.zeros((seq_count, seq_length, hidden_units), jnp.float32),
        jnp.zeros((seq_count, seq_length, hidden_units), jnp.bfloat16),
        jnp.zeros((seq_count, features), jnp.float32),
        jnp.zeros((seq_count, 1), jnp.float32),
    )


def local(
    images,
    captions,
    token_ids,
    counts,
    matches,
    image_weights,
    image_norms,
    weights,
    norm_params,
    momentum,
    norm_momentum,
    averages,
    norm_averages,
):
    tower_index = lax.axis_index("tower")
    seq_count, seq_length, features = captions.shape
    frozen = lax.all_gather(image_weights, "dp", axis=0, tiled=True)
    low_shard = weights.astype(jnp.bfloat16)
    packed = lax.all_gather(low_shard, ("tower", "dp"), axis=0, tiled=True)
    hidden_units = (packed.shape[0] - 4 * features) // 2

    def image_side(operand):
        block_out = block_forward(images.astype(jnp.float32), frozen, image_norms, False)[1]
        top_rows = block_out[:, 0]
        return (
            top_rows * lax.rsqrt(jnp.sum(top_rows * top_rows, axis=-1, keepdims=True) + EPSILON)
        ).astype(jnp.bfloat16)

    def image_blank(operand):
        return jnp.zeros((images.shape[0], features), jnp.bfloat16)

    pooled_image = lax.cond(tower_index == 0, image_side, image_blank, 0)
    crossed = passed_along(pooled_image, "tower", 1)
    every_image, every_count = (
        lax.all_gather(crossed, "dp", axis=0, tiled=True),
        lax.all_gather(counts.astype(jnp.bfloat16), "dp", axis=0, tiled=True),
    )
    tokens = captions.astype(jnp.float32)
    lengths = jnp.sum((token_ids != 0).astype(jnp.int32), axis=1)
    pool_mask = (
        lax.broadcasted_iota(jnp.int32, (seq_count, seq_length), 1) == (lengths - 1)[:, None]
    ).astype(jnp.float32)

    def text_side(operand):
        kept, block_out = block_forward(tokens, packed, norm_params, True)
        pooled_rows = jnp.sum(block_out * pool_mask[:, :, None], axis=1)
        inverse = lax.rsqrt(jnp.sum(pooled_rows * pooled_rows, axis=-1, keepdims=True) + EPSILON)
        return kept + (pooled_rows, inverse)

    def text_skip(operand):
        return text_blank(seq_count, seq_length, features, hidden_units)

    forward = lax.cond(tower_index == 1, text_side, text_skip, 0)
    pooled_rows, inverse = (forward[8], forward[9])
    text_emb = (pooled_rows * inverse).astype(jnp.bfloat16)
    logits = LOGIT_SCALE * jnp.einsum(
        "cd,id->ci", text_emb, every_image, preferred_element_type=jnp.float32
    )
    row_top = jnp.max(logits, axis=1, keepdims=True)
    row_lse = row_top + jnp.log(jnp.sum(jnp.exp(logits - row_top), axis=1, keepdims=True))
    all_text = lax.all_gather(text_emb, "dp", axis=0, tiled=True)
    own_logits = LOGIT_SCALE * jnp.einsum(
        "cd,id->ci", all_text, crossed, preferred_element_type=jnp.float32
    )
    own_top = jnp.max(own_logits, axis=0)
    own_lse = own_top + jnp.log(jnp.sum(jnp.exp(own_logits - own_top[None, :]), axis=0))
    column_lse = lax.all_gather(own_lse, "dp", axis=0, tiled=True)
    target = (matches[:, None] == lax.broadcasted_iota(jnp.int32, logits.shape, 1)).astype(
        jnp.float32
    )
    grad_logits = 0.5 * (jnp.exp(logits - row_lse) - target) + 0.5 * (
        jnp.exp(logits - column_lse[None, :]) - target / every_count.astype(jnp.float32)[None, :]
    )
    scaled_grad = (LOGIT_SCALE * grad_logits).astype(jnp.bfloat16)
    grad_embed = jnp.einsum(
        "ci,id->cd", scaled_grad, every_image, preferred_element_type=jnp.float32
    )
    projection = jnp.sum(pooled_rows * grad_embed, axis=-1, keepdims=True)
    grad_pooled = inverse * grad_embed - inverse * inverse * inverse * projection * pooled_rows
    grad_rows = pool_mask[:, :, None] * grad_pooled[:, None, :]

    def text_back(operand):
        return block_backward(grad_rows, tokens, packed, norm_params, forward[:8])

    def back_skip(operand):
        return (
            jnp.zeros(packed.shape, jnp.float32),
            jnp.zeros(norm_params.shape, jnp.float32),
            jnp.zeros(tokens.shape, jnp.float32),
        )

    raw_grads, raw_norm_grads, input_full = lax.cond(tower_index == 1, text_back, back_skip, 0)
    own_grads = lax.psum_scatter(raw_grads, ("tower", "dp"), scatter_dimension=0, tiled=True)
    total_norm_grads, square_total = lax.psum(
        (raw_norm_grads, jnp.sum(own_grads * own_grads)), ("tower", "dp")
    )
    grad_norm = jnp.sqrt(square_total + jnp.sum(total_norm_grads * total_norm_grads))
    factor = jnp.minimum(1.0, CLIP_NORM / (grad_norm + 1e-06))
    grads = own_grads * factor
    norm_grads = total_norm_grads * factor
    step_rate = 0.4 * math.sqrt(packed.shape[0])
    decayed = grads + DECAY_RATE * weights
    new_momentum = MOMENTUM_RATE * momentum + decayed
    new_weights = weights - step_rate * (decayed + MOMENTUM_RATE * new_momentum)
    new_averages = AVERAGE_RATE * averages + (1.0 - AVERAGE_RATE) * new_weights
    new_norm_momentum = MOMENTUM_RATE * norm_momentum + norm_grads
    new_norm_params = norm_params - step_rate * (norm_grads + MOMENTUM_RATE * new_norm_momentum)
    new_norm_averages = AVERAGE_RATE * norm_averages + (1.0 - AVERAGE_RATE) * new_norm_params
    half_width = features // 2
    given_half = passed_along(
        input_full[:, :, :half_width].astype(jnp.bfloat16), "tower", -1
    ).astype(jnp.float32)
    input_grad = jnp.where(tower_index == 0, given_half, input_full[:, :, half_width:])
    return (
        grads,
        norm_grads,
        input_grad,
        new_weights,
        new_momentum,
        new_averages,
        new_norm_params,
        new_norm_momentum,
        new_norm_averages,
        grad_norm,
    )


def solution(mesh):
    return jax.shard_map(
        local,
        mesh=mesh,
        in_specs=(
            P("dp", None, None),
            P("dp", None, None),
            P("dp", None),
            P("dp"),
            P("dp"),
            P("dp", None),
            P(),
            P(("tower", "dp"), None),
            P(),
            P(("tower", "dp"), None),
            P(),
            P(("tower", "dp"), None),
            P(),
        ),
        out_specs=(
            P(("tower", "dp"), None),
            P(),
            P("dp", None, "tower"),
            P(("tower", "dp"), None),
            P(("tower", "dp"), None),
            P(("tower", "dp"), None),
            P(),
            P(),
            P(),
            P(),
        ),
        check_vma=False,
    )
```

profile of v0, /device:TPU:0, one launch (start us, length us, event | category | flops | bytes accessed | tf_op | source)
XLA Modules:
  0.0 868.4 jit_solution(6323068292886722784)
XLA Ops:
  7.2 2.0 convert_element_type.135
  11.8 104.9 %all-gather.6.cloned.1.call-done = bf16[9216,768]{1,0:T(8,128)(2,1)} async-done(((bf16[288,768]{1,0:T(8,128)(2,1)}), bf16[9216,768]{1,0:T(8,128)(2,1)}) %all-gather.6.cloned.1.call-update) | async-done | bytes 14155792 | tf_op jit(solution)/shard_map/all_gather | solution.py:185
  116.7 28.0 %conditional.3 = (bf16[54,16,768]{2,1,0:T(8,128)(2,1)}, bf16[54,16,3,12,64]{4,3,2,1,0:T(8,128)(2,1)}, f32[54,12,16,1]{2,1,0,3:T(8,128)S(1)}, bf16[54,16,768]{2,1...) conditional(s32[]{:T(128)} %convert_element_type.133, () %tuple.33, ...), branch_computations={%region_1.2_spmd, %region_2.11_spmd} | conditional | flops 12316222464 | bytes 96540504 | solution.py:219
  120.9 1.8 broadcast.285
  122.7 3.0 broadcast.287
  125.7 6.4 broadcast.283
  132.2 5.2 broadcast.286
  146.6 80.9 %all-gather.8.cloned.1.call-done = bf16[9216,768]{1,0:T(8,128)(2,1)} async-done(((bf16[576,768]{1,0:T(8,128)(2,1)}), bf16[9216,768]{1,0:T(8,128)(2,1)}) %all-gather.8.cloned.1.call-update) | async-done | bytes 14155792 | tf_op jit(solution)/shard_map/all_gather | solution.py:183
  227.6 75.8 %conditional.4 = (bf16[18,768]{1,0:T(8,128)(2,1)S(1)}) conditional(s32[]{:T(128)} %convert_element_type.140, () %tuple.35, (bf16[18,50,768]{2,1,0:T(8,128)(2,1)}, f32[4,768]{1,0:T(4,128)S(1)}, bf16[9216,768]{1,0:T(8,128)(2,1)}) %tuple.93), branch_computations={%region_11.12_spmd, %region_12.20_spmd} | conditional | flops 12925296640 | bytes 90307072 | solution.py:198
  227.6 1.8 convert_reduce_fusion
  229.4 2.0 fusion.53
  231.5 8.0 convolution_convert_fusion.1
  239.4 11.5 %reshape.256 = bf16[18,50,3,12,64]{4,3,2,1,0:T(8,128)(2,1)} reshape(bf16[18,50,2304]{2,1,0:T(8,128)(2,1)} %convolution_convert_fusion.1) | data formatting | bytes 8294400 | tf_op jit(solution)/shard_map/cond/branch_1_fun/reshape | solution.py:61
  250.9 5.5 fusion.164
  258.2 10.1 %fusion.165 = (f32[18,12,50]{2,1,0:T(8,128)S(1)}, f32[18,12,50,50]{2,3,1,0:T(8,128)S(1)}) fusion(f32[18,12,50,50]{2,3,1,0:T(8,128)S(1)} %fusion.58), kind=kOutput, calls=%fused_computation.269 | output fusion | flops 2160049 | bytes 4363200 | tf_op jit(solution)/shard_map/cond/branch_1_fun/sub | solution.py:64
  268.2 1.8 convert_bitcast_fusion.1
  270.1 2.6 copy.79
  272.6 5.9 reshape.257
  278.5 3.8 fusion.166
  284.6 17.2 %fusion.39 = f32[18,50,768]{2,1,0:T(8,128)} fusion(bf16[9216,768]{1,0:T(8,128)(2,1)} %get-tuple-element.113, f32[18,50,768]{2,1,0:T(8,128)} %copy-done.10, f32[768]{0:T(1024)S(1)} %get-tuple-element.225, f32[768]{0:T(1024)S(1)} %get-tuple-element.222, f32[18,50]{1,0:T(8,128)S(1)} %add_rsqrt_fusion.2, f32[18,50]{1,0:T(8,128)S(1)} %broadcast_multiply_fusion.2), kind=kOutput, calls=%fused_computation.67 | convolution fusion | flops 8521804800 | bytes 15311904 | tf_op jit(solution)/shard_map/cond/branch_1_fun/nlf,fd->nld/dot_general | solution.py:78
  306.8 30.7 %all-reduce.1 = bf16[288]{0:T(512)(128)(2,1)S(1)} all-reduce(bf16[288]{0:T(512)(128)(2,1)S(1)} %dynamic-update-slice.1), channel_id=1, replica_groups=mesh['tower'=2,'dp'=16] {'dp'}, use_global_device_ids=true, to_apply=%add.1 | all-reduce | flops 288 | bytes 1152
  338.2 19.0 %all-gather = bf16[16,18,768]{2,1,0:T(8,128)(2,1)S(1)} all-gather(bf16[1,18,768]{2,1,0:T(8,128)(2,1)S(1)} %bitcast.168), channel_id=1, replica_groups=mesh['tower'=2,'dp'=16] {'dp'}, dimensions={0}, use_global_device_ids=true | all-gather | bytes 470016 | tf_op jit(solution)/shard_map/all_gather | solution.py:201
  361.0 2.4 reshape.268
  363.4 1.9 fusion.167
  365.6 31.7 %all-reduce = f32[288]{0:T(512)} all-reduce(f32[288]{0:T(512)S(1)} %add_dynamic-update-slice_fusion), channel_id=1, replica_groups=mesh['tower'=2,'dp'=16] {'dp'}, use_global_device_ids=true, to_apply=%add | all-reduce | flops 288 | bytes 2304
  399.3 12.9 %conditional.5 = (f32[9216,768]{1,0:T(8,128)}, f32[4,768]{1,0:T(4,128)}, f32[54,16,768]{2,1,0:T(8,128)S(1)}) conditional(s32[]{:T(128)} %convert_element_type.133, () %tuple.32, (bf16[54,16,3,12,64]{4,3,2,1,0:T(8,128)(2,1)}, f32[54,12,16,1]{2,1,0,3:T(8,128)S(1)}, f32[54,16,1]{1,0,2:T(8,128)}, f32[54,768]{1,0:T(8,128)S(1)}, ...), branch_computations={%region_24.25_spmd, %region_25.40_spmd} | conditional | flops 24696150016 | bytes 398636160 | solution.py:258
  400.2 9.5 %broadcast.307 = f32[9216,768]{1,0:T(8,128)} broadcast(f32[]{:T(128)} %constant.88.clone), dimensions={} | broadcast | bytes 28311556 | tf_op jit(solution)/shard_map/broadcast.59
  413.7 154.3 %collective-permute-done.1 = bf16[54,16,384]{2,1,0:T(8,128)(2,1)S(1)} collective-permute-done((bf16[54,16,384]{2,1,0:T(8,128)(2,1)S(1)}, bf16[54,16,384]{2,1,0:T(8,128)(2,1)S(1)}, u32[]{:S(2)}, u32[]{:S(2)}) %collective-permute-start.1) | collective-permute-done | bytes 663584 | tf_op jit(solution)/shard_map/ppermute | solution.py:20
  569.3 241.4 %reduce-scatter.2.cloned.1.call-done = f32[288,768]{1,0:T(8,128)} async-done(((f32[9216,768]{1,0:T(8,128)}), f32[288,768]{1,0:T(8,128)}) %reduce-scatter.2.cloned.1.call-update) | async-done | bytes 884752 | tf_op jit(solution)/shard_map/reduce_scatter | solution.py:259
  810.7 2.0 multiply_reduce_fusion.14
  812.7 40.5 %all-reduce.2 = (f32[]{:T(128)}, f32[4,768]{1,0:T(4,128)S(1)}) all-reduce(f32[]{:T(128)} %multiply_reduce_fusion.14, f32[4,768]{1,0:T(4,128)} %get-tuple-element.164), channel_id=1, replica_groups=mesh['tower'=2,'dp'=16] {'tower','dp'}, use_global_device_ids=true, to_apply=%region_42.0 | all-reduce | flops 3073 | bytes 24584 | tf_op jit(solution)/shard_map/psum | solution.py:260
  856.5 3.7 multiply_add_fusion.3
  (83 shorter events, 29.2 us)
Async XLA Ops:
  7.2 4.6 copy-start.23
  7.2 109.5 %copy-start.18 = (f32[4,768]{1,0:T(4,128)S(1)}, f32[4,768]{1,0:T(4,128)}, u32[]{:S(2)}) copy-start(f32[4,768]{1,0:T(4,128)} %param.27) | copy-start | bytes 36868
  7.2 109.5 %all-gather.6.cloned.1.call-start = ((), (), s32[]{:S(2)}) async-start(), calls=%async_computation.1 | async-start | bytes 14598144 | tf_op jit(solution)/shard_map/all_gather | solution.py:185
  9.2 218.3 %all-gather.8.cloned.1.call-start = ((), (), s32[]{:S(2)}) async-start(), calls=%async_computation.2 | async-start | bytes 15040512 | tf_op jit(solution)/shard_map/all_gather | solution.py:183
  10.0 351.0 %all-gather.10.cloned.1.call-start = ((), (), s32[]{:S(2)}) async-start(), calls=%async_computation.4 | async-start | bytes 1462272 | tf_op jit(solution)/shard_map/all_gather | solution.py:227
  116.7 110.9 %copy-start.20 = (f32[4,768]{1,0:T(4,128)S(1)}, f32[4,768]{1,0:T(4,128)}, u32[]{:S(2)}) copy-start(f32[4,768]{1,0:T(4,128)} %param.25) | copy-start | bytes 36868
  144.7 82.8 %copy-start.13 = (f32[54,12,16,1]{2,1,0,3:T(8,128)}, f32[54,12,16,1]{2,1,0,3:T(8,128)S(1)}, u32[]{:S(2)}) copy-start(f32[54,12,16,1]{2,1,0,3:T(8,128)S(1)} %get-tuple-element.154) | copy-start | bytes 124420
  144.8 213.3 %copy-start.24 = (f32[54,1]{0,1:T(1,128)}, f32[54,1]{0,1:T(1,128)S(1)}, u32[]{:S(2)}) copy-start(f32[54,1]{0,1:T(1,128)S(1)} %get-tuple-element.155) | copy-start | bytes 652
  146.6 664.1 %reduce-scatter.2.cloned.1.call-start = ((), (), s32[]{:S(2)}) async-start(), calls=%async_computation.3 | async-start | bytes 29196288 | tf_op jit(solution)/shard_map/reduce_scatter | solution.py:259
  227.6 77.8 %copy-start.25 = (s32[18]{0:T(128)S(1)}, s32[18]{0:T(128)}, u32[]{:S(2)}) copy-start(s32[18]{0:T(128)} %param.22) | copy-start | bytes 220
  227.6 77.8 %copy-start.26 = (u32[32]{0:T(128)S(1)}, u32[32]{0:T(128)}, u32[]{:S(2)}) copy-start(u32[32]{0:T(128)} %constant.158) | copy-start | bytes 388
  227.6 3.9 copy-start.7
  282.3 1.7 copy-start.10
  303.4 34.8 %collective-permute-start = (bf16[18,768]{1,0:T(8,128)(2,1)S(1)}, bf16[18,768]{1,0:T(8,128)(2,1)S(1)}, u32[]{:S(2)}, u32[]{:S(2)}) collective-permute-start(bf16[18,768]{1,0:T(8,128)(2,1)S(1)} %get-tuple-element.300), channel_id=1, source_target_pairs={{0,16},{1,17},{2,18},{3,19},{4,20},{5,21},{6,22},{7,23},{8,24},{9,... | collective-permute-start | bytes 82952 | tf_op jit(solution)/shard_map/ppermute | solution.py:20
  338.2 19.0 %copy-start.16 = (bf16[18,768]{1,0:T(8,128)(2,1)}, bf16[18,768]{1,0:T(8,128)(2,1)S(1)}, u32[]{:S(2)}) copy-start(bf16[18,768]{1,0:T(8,128)(2,1)S(1)} %collective-permute-done) | copy-start | bytes 82948
  358.1 39.2 %copy-start.12 = (bf16[288,768]{1,0:T(8,128)(2,1)S(1)}, bf16[288,768]{1,0:T(8,128)(2,1)}, u32[]{:S(2)}) copy-start(bf16[288,768]{1,0:T(8,128)(2,1)} %reshape.266) | copy-start | bytes 1327108
  358.1 41.2 %copy-start.14 = (f32[54,12,16,1]{2,1,0,3:T(8,128)S(1)}, f32[54,12,16,1]{2,1,0,3:T(8,128)}, u32[]{:S(2)}) copy-start(f32[54,12,16,1]{2,1,0,3:T(8,128)} %copy-done.13) | copy-start | bytes 124420
  359.6 0.6 copy-start.15
  412.2 444.4 %copy-start.9 = (f32[288,768]{1,0:T(8,128)S(1)}, f32[288,768]{1,0:T(8,128)}, u32[]{:S(2)}) copy-start(f32[288,768]{1,0:T(8,128)} %param.26) | copy-start | bytes 2654212
  412.3 155.8 %collective-permute-start.1 = (bf16[54,16,384]{2,1,0:T(8,128)(2,1)S(1)}, bf16[54,16,384]{2,1,0:T(8,128)(2,1)S(1)}, u32[]{:S(2)}, u32[]{:S(2)}) collective-permute-start(bf16[54,16,384]{2,1,0:T(8,128)(2,1)S(1)} %slice.206), channel_id=1, source_target_pairs={{16,0},{17,1},{18,2},{19,3},{20,4},{21,5},{22,6},{23,7},{24,8},{25... | collective-permute-start | bytes 1990664 | tf_op jit(solution)/shard_map/ppermute | solution.py:20
Sparse Core Ops, SparseCore 0:
  11.5 105.1 all-gather.5
  119.0 108.5 all-gather.7
  229.7 37.0 all-gather.9
  412.3 398.3 reduce-scatter.1
where the time goes:
time: 876 us; the launch traced here: 868 us
  waiting for transfers between devices  582 us (66%)
  blocking collectives  122 us (14%)
  local copies, waits for them, and re-layouts  63.9 us (7%)
  matrix products  37.2 us (4%)
  other arithmetic  32.5 us (4%)
  between operations  17.6 us (2%)
  loops' own time  10.1 us (1%)
    reduce_scatter x1, waiting for transfers between devices, local(): lax.psum_scatter(raw_grads, ('tower', 'dp'), scatter_dimension=0, tiled=T...  241 us
    ppermute x2, waiting for transfers between devices, passed_along(): return lax.ppermute(block, axis, route)  154 us
    all_gather x1, waiting for transfers between devices, local(): packed = lax.all_gather(low_shard, ('tower', 'dp'), axis=0, tiled=True)  105 us
    all_gather x1, waiting for transfers between devices, local(): frozen = lax.all_gather(image_weights, 'dp', axis=0, tiled=True)  80.9 us
    unnamed x2, blocking collectives  62.4 us
    psum x1, blocking collectives, local(): lax.psum((raw_norm_grads, jnp.sum(own_grads * own_grads)), ('tower', 'dp'))  40.5 us
    another operation x13, local copies, waits for them, and re-layouts  31.1 us
    all_gather x1, blocking collectives, local(): lax.all_gather(crossed, 'dp', axis=0, tiled=True)  19 us
  transfers between devices with their start and end apart: 6, of which 4 were waited for; matrix products, arithmetic and copies ran while one was open for 12% of the time, Pallas kernels for 0%

commit v1 on v0

--- a/solution.py
+++ b/solution.py
@@ -12,6 +12,31 @@
 MOMENTUM_RATE = 0.9
 DECAY_RATE = 0.0001
 AVERAGE_RATE = 0.7
+
+
+def begin_face(message):
+    net_axis = "dp"
+    after = lax.axis_index(net_axis)
+    arr_now = lax.axis_size(net_axis)
+    now, x_now, heard = (arr_now, after, message.shape[0])
+    steps_seen = [dev_i * now if ii == 0 else dev_i for ii, dev_i in enumerate(message.shape)]
+    inter = seen_now = message
+    it = 1
+    left_arr = lax.dynamic_update_slice_in_dim(
+        jnp.zeros(steps_seen, message.dtype), message, x_now * heard, axis=0
+    )
+    while it < now // 2 + 1:
+        inter = lax.ppermute(inter, net_axis, [(ii, (ii + 1) % now) for ii in range(now)])
+        left_arr = lax.dynamic_update_slice_in_dim(
+            left_arr, inter, (x_now - it) % now * heard, axis=0
+        )
+        if 2 * it < now:
+            seen_now = lax.ppermute(seen_now, net_axis, [(ii, (ii - 1) % now) for ii in range(now)])
+            left_arr = lax.dynamic_update_slice_in_dim(
+                left_arr, seen_now, (x_now + it) % now * heard, axis=0
+            )
+        it += 1
+    return left_arr
 
 
 def passed_along(block, axis, distance):
@@ -198,7 +223,7 @@
     pooled_image = lax.cond(tower_index == 0, image_side, image_blank, 0)
     crossed = passed_along(pooled_image, "tower", 1)
     every_image, every_count = (
-        lax.all_gather(crossed, "dp", axis=0, tiled=True),
+        begin_face(crossed),
         lax.all_gather(counts.astype(jnp.bfloat16), "dp", axis=0, tiled=True),
     )
     tokens = captions.astype(jnp.float32)

time: 876 us -> 952 us (1.087)
  waiting for transfers between devices: 582 us -> 627 us
  starting transfers between devices: 2.88 us -> 30.1 us
  local copies, waits for them, and re-layouts: 63.9 us -> 84.7 us
  blocking collectives: 122 us -> 105 us
    ppermute x2, waiting for transfers between devices: 154 us -> 188 us  [passed_along(): return lax.ppermute(block, axis, route)]
    ppermute x0 -> x15, starting transfers between devices: none -> 27.2 us  [the longest x7 27.2 us: begin_face(): lax.ppermute(seen_now, net_axis, [(ii, (ii - 1) % now) for ii in range(no...]
    all_gather x1 -> x0, blocking collectives: 19 us -> none  [local(): lax.all_gather(crossed, 'dp', axis=0, tiled=True)]
    dynamic_update_slice x0 -> x16, local copies, waits for them, and re-layouts: none -> 17.6 us  [the longest x8 8.77 us: begin_face(): lax.dynamic_update_slice_in_dim(left_arr, inter, (x_now - it) % now * hea...]
    ppermute x0 -> x15, waiting for transfers between devices: none -> 11.5 us  [the longest x8 11.3 us: begin_face(): lax.ppermute(inter, net_axis, [(ii, (ii + 1) % now) for ii in range(now)])]
  transfers between devices with their start and end apart: 6 -> 21, of which waited for: 4 -> 12; matrix products, arithmetic and copies ran while one was open for 12% -> 13% of each run, Pallas kernels for 0% -> 0%
where the time goes in v1:
time: 952 us; the launch traced here: 944 us
  waiting for transfers between devices  627 us (66%)
  blocking collectives  105 us (11%)
  local copies, waits for them, and re-layouts  84.7 us (9%)
  matrix products  37 us (4%)
  other arithmetic  32.3 us (3%)
  starting transfers between devices  30.1 us (3%)
  between operations  17.5 us (2%)
  loops' own time  10.3 us (1%)
    reduce_scatter x1, waiting for transfers between devices, local(): lax.psum_scatter(raw_grads, ('tower', 'dp'), scatter_dimension=0, tiled=T...  241 us
    ppermute x2, waiting for transfers between devices, passed_along(): return lax.ppermute(block, axis, route)  188 us
    all_gather x1, waiting for transfers between devices, local(): packed = lax.all_gather(low_shard, ('tower', 'dp'), axis=0, tiled=True)  105 us
    all_gather x1, waiting for transfers between devices, local(): frozen = lax.all_gather(image_weights, 'dp', axis=0, tiled=True)  81 us
    unnamed x2, blocking collectives  64 us
    psum x1, blocking collectives, local(): lax.psum((raw_norm_grads, jnp.sum(own_grads * own_grads)), ('tower', 'dp'))  40.5 us
    another operation x13, local copies, waits for them, and re-layouts  31.1 us
    ppermute x7, starting transfers between devices, begin_face(): lax.ppermute(seen_now, net_axis, [(ii, (ii - 1) % now) for ii in range(no...  27.2 us
  transfers between devices with their start and end apart: 21, of which 12 were waited for; matrix products, arithmetic and copies ran while one was open for 13% of the time, Pallas kernels for 0%

profile of v1, /device:TPU:0, one launch (start us, length us, event | category | flops | bytes accessed | tf_op | source)
XLA Modules:
  0.0 943.6 jit_solution(10643524577696960094)
XLA Ops:
  11.8 104.9 %all-gather.5.cloned.1.call-done = bf16[9216,768]{1,0:T(8,128)(2,1)} async-done(((bf16[288,768]{1,0:T(8,128)(2,1)}), bf16[9216,768]{1,0:T(8,128)(2,1)}) %all-gather.5.cloned.1.call-update) | async-done | bytes 14155792 | tf_op jit(solution)/shard_map/all_gather | solution.py:210
  116.7 28.1 %conditional.3 = (bf16[54,16,768]{2,1,0:T(8,128)(2,1)}, bf16[54,16,3,12,64]{4,3,2,1,0:T(8,128)(2,1)}, f32[54,12,16,1]{2,1,0,3:T(8,128)S(1)}, bf16[54,16,768]{2,1...) conditional(s32[]{:T(128)} %convert_element_type.133, () %tuple.33, ...), branch_computations={%region_1.2_spmd, %region_2.11_spmd} | conditional | flops 12316222464 | bytes 96540504 | solution.py:244
  122.7 3.0 broadcast.302
  125.7 6.4 broadcast.298
  132.2 5.2 broadcast.301
  146.6 81.0 %all-gather.7.cloned.1.call-done = bf16[9216,768]{1,0:T(8,128)(2,1)} async-done(((bf16[576,768]{1,0:T(8,128)(2,1)}), bf16[9216,768]{1,0:T(8,128)(2,1)}) %all-gather.7.cloned.1.call-update) | async-done | bytes 14155792 | tf_op jit(solution)/shard_map/all_gather | solution.py:208
  227.6 75.7 %conditional.4 = (bf16[18,768]{1,0:T(8,128)(2,1)S(1)}) conditional(s32[]{:T(128)} %convert_element_type.140, () %tuple.35, (bf16[18,50,768]{2,1,0:T(8,128)(2,1)}, f32[4,768]{1,0:T(4,128)S(1)}, bf16[9216,768]{1,0:T(8,128)(2,1)}) %tuple.92), branch_computations={%region_11.12_spmd, %region_12.20_spmd} | conditional | flops 12925296640 | bytes 90307072 | solution.py:223
  231.4 8.0 convolution_convert_fusion.1
  239.4 11.5 %reshape.256 = bf16[18,50,3,12,64]{4,3,2,1,0:T(8,128)(2,1)} reshape(bf16[18,50,2304]{2,1,0:T(8,128)(2,1)} %convolution_convert_fusion.1) | data formatting | bytes 8294400 | tf_op jit(solution)/shard_map/cond/branch_1_fun/reshape | solution.py:86
  250.8 5.5 fusion.164
  258.1 10.1 %fusion.165 = (f32[18,12,50]{2,1,0:T(8,128)S(1)}, f32[18,12,50,50]{2,3,1,0:T(8,128)S(1)}) fusion(f32[18,12,50,50]{2,3,1,0:T(8,128)S(1)} %fusion.58), kind=kOutput, calls=%fused_computation.269 | output fusion | flops 2160049 | bytes 4363200 | tf_op jit(solution)/shard_map/cond/branch_1_fun/sub | solution.py:89
  270.0 2.5 copy.79
  272.6 5.9 reshape.257
  278.4 3.8 fusion.166
  284.5 17.2 %fusion.39 = f32[18,50,768]{2,1,0:T(8,128)} fusion(bf16[9216,768]{1,0:T(8,128)(2,1)} %get-tuple-element.113, f32[18,50,768]{2,1,0:T(8,128)} %copy-done.10, f32[768]{0:T(1024)S(1)} %get-tuple-element.225, f32[768]{0:T(1024)S(1)} %get-tuple-element.222, f32[18,50]{1,0:T(8,128)S(1)} %add_rsqrt_fusion.2, f32[18,50]{1,0:T(8,128)S(1)} %broadcast_multiply_fusion.2), kind=kOutput, calls=%fused_computation.67 | convolution fusion | flops 8521804800 | bytes 15311904 | tf_op jit(solution)/shard_map/cond/branch_1_fun/nlf,fd->nld/dot_general | solution.py:103
  306.8 3.8 collective-permute-start.2
  312.9 3.9 collective-permute-start.4
  319.0 3.9 collective-permute-start.6
  325.1 3.9 collective-permute-start.8
  331.2 3.9 collective-permute-start.10
  337.2 3.9 collective-permute-start.12
  343.4 3.9 collective-permute-start.14
  351.2 33.9 %all-reduce.1 = bf16[288]{0:T(512)(128)(2,1)S(1)} all-reduce(bf16[288]{0:T(512)(128)(2,1)S(1)} %dynamic-update-slice.1), channel_id=1, replica_groups=mesh['tower'=2,'dp'=16] {'dp'}, use_global_device_ids=true, to_apply=%add.1 | all-reduce | flops 288 | bytes 1152
  406.2 2.4 reshape.266
  410.8 30.0 %all-reduce = f32[288]{0:T(512)} all-reduce(f32[288]{0:T(512)S(1)} %add_dynamic-update-slice_fusion), channel_id=1, replica_groups=mesh['tower'=2,'dp'=16] {'dp'}, use_global_device_ids=true, to_apply=%add | all-reduce | flops 288 | bytes 2304
  442.8 13.0 %conditional.5 = (f32[9216,768]{1,0:T(8,128)}, f32[4,768]{1,0:T(4,128)}, f32[54,16,768]{2,1,0:T(8,128)S(1)}) conditional(s32[]{:T(128)} %convert_element_type.133, () %tuple.32, (bf16[54,16,3,12,64]{4,3,2,1,0:T(8,128)(2,1)}, f32[54,12,16,1]{2,1,0,3:T(8,128)S(1)}, f32[54,16,1]{1,0,2:T(8,128)}, f32[54,768]{1,0:T(8,128)S(1)}, ...), branch_computations={%region_24.25_spmd, %region_25.40_spmd} | conditional | flops 24696150016 | bytes 398636160 | solution.py:283
  443.7 9.5 %broadcast.322 = f32[9216,768]{1,0:T(8,128)} broadcast(f32[]{:T(128)} %constant.207.clone), dimensions={} | broadcast | bytes 28311556 | tf_op jit(solution)/shard_map/broadcast.59
  457.4 186.8 %collective-permute-done.16 = bf16[54,16,384]{2,1,0:T(8,128)(2,1)S(1)} collective-permute-done((bf16[54,16,384]{2,1,0:T(8,128)(2,1)S(1)}, bf16[54,16,384]{2,1,0:T(8,128)(2,1)S(1)}, u32[]{:S(2)}, u32[]{:S(2)}) %collective-permute-start.16) | collective-permute-done | bytes 663584 | tf_op jit(solution)/shard_map/ppermute | solution.py:45
  645.4 240.7 %reduce-scatter.2.cloned.1.call-done = f32[288,768]{1,0:T(8,128)} async-done(((f32[9216,768]{1,0:T(8,128)}), f32[288,768]{1,0:T(8,128)}) %reduce-scatter.2.cloned.1.call-update) | async-done | bytes 884752 | tf_op jit(solution)/shard_map/reduce_scatter | solution.py:284
  886.1 2.0 multiply_reduce_fusion.14
  888.1 40.5 %all-reduce.2 = (f32[]{:T(128)}, f32[4,768]{1,0:T(4,128)S(1)}) all-reduce(f32[]{:T(128)} %multiply_reduce_fusion.14, f32[4,768]{1,0:T(4,128)} %get-tuple-element.164), channel_id=1, replica_groups=mesh['tower'=2,'dp'=16] {'tower','dp'}, use_global_device_ids=true, to_apply=%region_42.43 | all-reduce | flops 3073 | bytes 24584 | tf_op jit(solution)/shard_map/psum | solution.py:285
  932.0 3.7 multiply_add_fusion.3
  (144 shorter events, 74.1 us)
Async XLA Ops:
  7.2 109.5 %copy-start.15 = (f32[4,768]{1,0:T(4,128)S(1)}, f32[4,768]{1,0:T(4,128)}, u32[]{:S(2)}) copy-start(f32[4,768]{1,0:T(4,128)} %param.27) | copy-start | bytes 36868
  7.2 109.5 %all-gather.5.cloned.1.call-start = ((), (), s32[]{:S(2)}) async-start(), calls=%async_computation.1 | async-start | bytes 14598144 | tf_op jit(solution)/shard_map/all_gather | solution.py:210
  9.2 218.3 %all-gather.7.cloned.1.call-start = ((), (), s32[]{:S(2)}) async-start(), calls=%async_computation.2 | async-start | bytes 15040512 | tf_op jit(solution)/shard_map/all_gather | solution.py:208
  10.0 396.2 %all-gather.9.cloned.1.call-start = ((), (), s32[]{:S(2)}) async-start(), calls=%async_computation.4 | async-start | bytes 1462272 | tf_op jit(solution)/shard_map/all_gather | solution.py:252
  116.7 110.9 %copy-start.28 = (f32[4,768]{1,0:T(4,128)S(1)}, f32[4,768]{1,0:T(4,128)}, u32[]{:S(2)}) copy-start(f32[4,768]{1,0:T(4,128)} %param.25) | copy-start | bytes 36868
  144.9 258.7 %copy-start.32 = (f32[54,1]{0,1:T(1,128)}, f32[54,1]{0,1:T(1,128)S(1)}, u32[]{:S(2)}) copy-start(f32[54,1]{0,1:T(1,128)S(1)} %get-tuple-element.155) | copy-start | bytes 652
  146.5 739.6 %reduce-scatter.2.cloned.1.call-start = ((), (), s32[]{:S(2)}) async-start(), calls=%async_computation.3 | async-start | bytes 29196288 | tf_op jit(solution)/shard_map/reduce_scatter | solution.py:284
  227.6 122.1 %copy-start.33 = (s32[18]{0:T(128)S(1)}, s32[18]{0:T(128)}, u32[]{:S(2)}) copy-start(s32[18]{0:T(128)} %param.22) | copy-start | bytes 220
  227.6 122.1 %copy-start.34 = (u32[32]{0:T(128)S(1)}, u32[32]{0:T(128)}, u32[]{:S(2)}) copy-start(u32[32]{0:T(128)} %constant.263) | copy-start | bytes 388
  303.3 2.9 collective-permute-start
  306.2 6.1 collective-permute-start.1
  306.8 5.5 collective-permute-start.2
  312.3 6.1 collective-permute-start.3
  312.9 5.5 copy-start.18
  312.9 5.5 collective-permute-start.4
  318.4 6.1 collective-permute-start.5
  319.0 5.5 copy-start.20
  319.0 5.5 collective-permute-start.6
  324.5 6.1 collective-permute-start.7
  325.1 5.5 copy-start.22
  325.1 5.5 collective-permute-start.8
  330.5 6.1 collective-permute-start.9
  331.2 5.5 copy-start.24
  331.2 5.5 collective-permute-start.10
  336.6 6.2 collective-permute-start.11
  337.2 5.6 copy-start.26
  337.2 5.6 collective-permute-start.12
  342.8 6.2 collective-permute-start.13
  343.4 57.9 %collective-permute-start.14 = (bf16[18,768]{1,0:T(8,128)(2,1)}, bf16[18,768]{1,0:T(8,128)(2,1)}, u32[]{:S(2)}, u32[]{:S(2)}) collective-permute-start(bf16[18,768]{1,0:T(8,128)(2,1)} %collective-permute-done.12), channel_id=1, source_target_pairs={{0,15},{1,0},{2,1},{3,2},{4,3},{5,4},{6,5},{7,6},{8,7},{9,8},{10,9... | collective-permute-start | bytes 82952 | tf_op jit(solution)/shard_map/ppermute | solution.py:34
  349.0 53.4 %collective-permute-start.15 = (bf16[18,768]{1,0:T(8,128)(2,1)}, bf16[18,768]{1,0:T(8,128)(2,1)}, u32[]{:S(2)}, u32[]{:S(2)}) collective-permute-start(bf16[18,768]{1,0:T(8,128)(2,1)} %collective-permute-done.13), channel_id=1, source_target_pairs={{0,1},{1,2},{2,3},{3,4},{4,5},{5,6},{6,7},{7,8},{8,9},{9,10},{10,1... | collective-permute-start | bytes 82952 | tf_op jit(solution)/shard_map/ppermute | solution.py:29
  455.8 476.2 %copy-start.9 = (f32[288,768]{1,0:T(8,128)S(1)}, f32[288,768]{1,0:T(8,128)}, u32[]{:S(2)}) copy-start(f32[288,768]{1,0:T(8,128)} %param.26) | copy-start | bytes 2654212
  455.9 188.2 %collective-permute-start.16 = (bf16[54,16,384]{2,1,0:T(8,128)(2,1)S(1)}, bf16[54,16,384]{2,1,0:T(8,128)(2,1)S(1)}, u32[]{:S(2)}, u32[]{:S(2)}) collective-permute-start(bf16[54,16,384]{2,1,0:T(8,128)(2,1)S(1)} %slice.206), channel_id=1, source_target_pairs={{16,0},{17,1},{18,2},{19,3},{20,4},{21,5},{22,6},{23,7},{24,8},{25... | collective-permute-start | bytes 1990664 | tf_op jit(solution)/shard_map/ppermute | solution.py:45
  (11 other events, 15.1 us)
Sparse Core Ops, SparseCore 0:
  11.5 105.1 all-gather.4
  119.0 108.5 all-gather.6
  230.3 37.1 all-gather.8
  455.9 430.1 reduce-scatter.1
